TPU v7x, 32 devices: a whole 2x2x4 slice. The times are simulated.
32 devices in a mesh: src: 16 (over z, y, core), tgt: 2 (over x).
Axes of the slice: x: 2, y: 2, z: 4, core: 2. Of those that a mesh axis runs over, the one named last changes fastest.
Arguments:
- inputs: bfloat16 [64, 2, 1024, 512], P(('src', 'tgt')), may hold values from -6 to 6
- leaf_maps: bfloat16 [64, 2, 256, 1024], P(('src', 'tgt')), may hold values from -0.125 to 0.125
- transfer_blocks: bfloat16 [4, 64, 2, 2, 256, 256], P(None, ('src', 'tgt')), may hold values from -0.1875 to 0.1875
Outputs:
- butterfly_out: bfloat16 [64, 2, 256, 512], P(('src', 'tgt'))
All inputs are finite; a program needn't handle non-finite values.
Results may differ from a plain program's by a relative error of at most 0.012.
Values may be sent and summed in bfloat16 or wider, within the bound.
A program may use at most 64 MiB of HBM per device.

v0:
```python
import functools

import jax
import jax.numpy as jnp
from jax import lax
from jax.experimental import pallas as pl
from jax.experimental.pallas import tpu as pltpu
from jax.sharding import PartitionSpec as P

MESH = pl.DeviceIdType.MESH
LANES = 128


def product(blocks, vectors):
    rows = blocks.shape[0] // 2
    width = vectors.shape[1] // 2
    both = jnp.dot(blocks, vectors, preferred_element_type=jnp.float32)
    real_part = both[:rows, :width] - both[rows:, width:]
    imag_part = both[:rows, width:] + both[rows:, :width]
    return jnp.concatenate([real_part, imag_part], axis=1)


def kernel(
    sizes,
    inputs,
    leaf_maps,
    transfer,
    out,
    x_in,
    maps,
    blocks,
    coeffs,
    send1,
    relay_a,
    relay_b,
    recv1,
    send2,
    recv2,
    send3,
    recv3,
    result,
    in_sem,
    maps_sem,
    blocks_sem,
    out_sem,
    s1_sem,
    ra_sem,
    rb_sem,
    fa_sem,
    fb_sem,
    r1_sem,
    s2_sem,
    r2_sem,
    s3_sem,
    r3_sem,
):
    src_bits, tgt_bits, levels, chunks = sizes
    units = 2 * chunks
    src, tgt = lax.axis_index("src"), lax.axis_index("tgt")
    hi, lo = 2 ** (src_bits - 1), 2 ** (src_bits - 2)
    far = 2 ** (tgt_bits - 1)
    bit1, bit2, bit3 = src // hi % 2, src // lo % 2, tgt // far % 2
    flip_lo = src + lo - 2 * lo * bit2
    flip_both = flip_lo + hi - 2 * hi * bit1
    near = (flip_lo, tgt)
    across = (flip_both, tgt)
    side = (src, tgt + far - 2 * far * bit3)
    is_end = bit1 == bit2
    is_mid = bit1 != bit2

    barrier = pltpu.get_barrier_semaphore()
    for peer in (near, across, side):
        pl.semaphore_signal(barrier, inc=1, device_id=peer, device_id_type=MESH)

    def load_in(c, n, part):
        return pltpu.make_async_copy(
            inputs.at[n, part, :, pl.ds(pl.multiple_of(c * LANES, LANES), LANES)],
            x_in.at[c, n, :, pl.ds(part * LANES, LANES)],
            in_sem.at[c, n, part],
        )

    def load_maps(n):
        return pltpu.make_async_copy(leaf_maps.at[n], maps.at[n], maps_sem.at[n])

    def load_blocks(v):
        return pltpu.make_async_copy(transfer.at[v], blocks.at[v], blocks_sem.at[v])

    for n in range(2):
        load_maps(n).start()
        for part in range(2):
            load_in(0, n, part).start()
    load_blocks(0).start()
    load_blocks(1).start()
    for c in range(1, chunks):
        for n in range(2):
            for part in range(2):
                load_in(c, n, part).start()
    for v in range(2, levels):
        load_blocks(v).start()

    def remote(source, target, send_sem, recv_sem, peer):
        return pltpu.make_async_remote_copy(
            src_ref=source,
            dst_ref=target,
            send_sem=send_sem,
            recv_sem=recv_sem,
            device_id=peer,
            device_id_type=MESH,
        )

    def own_a(u):
        return remote(send1.at[u], relay_a.at[u], s1_sem.at[u], ra_sem.at[u], near)

    def own_b(u):
        return remote(send1.at[u], relay_b.at[u], s1_sem.at[u], rb_sem.at[u], across)

    def forward_a(u):
        return remote(relay_a.at[u], recv1.at[u], fa_sem.at[u], r1_sem.at[u], across)

    def forward_b(u):
        return remote(relay_b.at[u], recv1.at[u], fb_sem.at[u], r1_sem.at[u], near)

    def second(u):
        return remote(send2.at[u], recv2.at[u], s2_sem.at[u], r2_sem.at[u], near)

    def third(u):
        return remote(send3.at[u], recv3.at[u], s3_sem.at[u], r3_sem.at[u], side)

    def forward(u):
        own_b(u).wait_recv()
        forward_b(u).start()
        own_a(u).wait_recv()
        forward_a(u).start()

    def store(u, part):
        return pltpu.make_async_copy(
            result.at[u, :, pl.ds(part * LANES, LANES)],
            out.at[u % 2, part, :, pl.ds(pl.multiple_of(u // 2 * LANES, LANES), LANES)],
            out_sem.at[u, part],
        )

    def pre(c):
        vectors = []
        for n in range(2):
            for part in range(2):
                load_in(c, n, part).wait()
            vectors.append(product(maps[n], x_in[c, n]).astype(jnp.bfloat16))

        @pl.when(c == 0)
        def _():
            load_blocks(0).wait()
            load_blocks(1).wait()

        for n in range(2):
            own_term = product(blocks[0, n, n], vectors[n])
            partner = product(blocks[0, 1 - n, n], vectors[1 - n]).astype(jnp.bfloat16)
            updated = (own_term + partner.astype(jnp.float32)).astype(jnp.bfloat16)
            u = 2 * c + n
            coeffs[u] = updated
            send1[u] = product(blocks[1, n, 1 - bit1], updated).astype(jnp.bfloat16)
            if n == 0:

                @pl.when(c == 0)
                def _():
                    pl.semaphore_wait(barrier, 3)

            @pl.when(is_end)
            def _():
                own_a(u).start()

            @pl.when(is_mid)
            def _():
                own_b(u).start()

    def level(v, u, bit, arrived):
        local_term = product(blocks[v, u % 2, bit], coeffs[u])
        return (local_term + arrived[u].astype(jnp.float32)).astype(jnp.bfloat16)

    def post1(u):
        forward_a(u).wait_recv()
        updated = level(1, u, bit1, recv1)
        coeffs[u] = updated
        send2[u] = product(blocks[2, u % 2, 1 - bit2], updated).astype(jnp.bfloat16)
        second(u).start()

    def post2(u):
        second(u).wait_recv()
        updated = level(2, u, bit2, recv2)
        coeffs[u] = updated
        send3[u] = product(blocks[3, u % 2, 1 - bit3], updated).astype(jnp.bfloat16)
        third(u).start()

    def post3(u):
        third(u).wait_recv()
        result[u] = level(3, u, bit3, recv3)
        for part in range(2):
            store(u, part).start()

    for n in range(2):
        load_maps(n).wait()

    @pl.loop(0, chunks)
    def _(c):
        pre(c)

        @pl.when(jnp.logical_and(is_mid, c > 0))
        def _():
            forward(c - 1)

    for v in range(2, levels):
        load_blocks(v).wait()

    @pl.when(is_mid)
    def _():
        @pl.loop(chunks - 1, units)
        def _(u):
            forward(u)

    @pl.when(is_end)
    def _():
        @pl.loop(0, units)
        def _(u):
            post1(u)

    @pl.loop(0, units + 2)
    def _(u):
        @pl.when(jnp.logical_and(is_mid, u < units))
        def _():
            post1(u)

        @pl.when(jnp.logical_and(u >= 1, u < units + 1))
        def _():
            post2(u - 1)

        @pl.when(u >= 2)
        def _():
            post3(u - 2)

    @pl.loop(0, units)
    def _(u):
        own_a(u).wait_send()
        second(u).wait_send()
        third(u).wait_send()
        for part in range(2):
            store(u, part).wait()

        @pl.when(is_mid)
        def _():
            forward_a(u).wait_send()
            forward_b(u).wait_send()


def local(inputs, leaf_maps, transfer_blocks):
    nodes, _, depth, columns = inputs.shape
    rank = leaf_maps.shape[2]
    levels = transfer_blocks.shape[0]
    chunks = columns // LANES
    units = nodes * chunks
    src_bits = lax.axis_size("src").bit_length() - 1
    tgt_bits = lax.axis_size("tgt").bit_length() - 1
    maps = leaf_maps.reshape(nodes, 2 * rank, depth)
    blocks = transfer_blocks.reshape(levels, nodes, 2, 2 * rank, rank)
    unit = pltpu.VMEM((units, rank, 2 * LANES), jnp.bfloat16)
    dma = pltpu.SemaphoreType.DMA
    return pl.pallas_call(
        functools.partial(kernel, (src_bits, tgt_bits, levels, chunks)),
        out_shape=jax.ShapeDtypeStruct((nodes, 2, rank, columns), jnp.bfloat16),
        in_specs=[pl.BlockSpec(memory_space=pl.ANY)] * 3,
        out_specs=pl.BlockSpec(memory_space=pl.ANY),
        scratch_shapes=[
            pltpu.VMEM((chunks, nodes, depth, 2 * LANES), jnp.bfloat16),
            pltpu.VMEM(maps.shape, jnp.bfloat16),
            pltpu.VMEM(blocks.shape, jnp.bfloat16),
        ]
        + [unit] * 10
        + [
            dma((chunks, nodes, 2)),
            dma((nodes,)),
            dma((levels,)),
            dma((units, 2)),
        ]
        + [dma((units,))] * 10,
        compiler_params=pltpu.CompilerParams(
            collective_id=0, has_side_effects=True, vmem_limit_bytes=60 * 2**20
        ),
    )(inputs, maps, blocks)


def solution(mesh):
    placed = (
        P(("src", "tgt"), None, None, None),
        P(("src", "tgt"), None, None, None),
        P(None, ("src", "tgt"), None, None, None, None),
    )
    return jax.shard_map(
        local,
        mesh=mesh,
        in_specs=placed,
        out_specs=P(("src", "tgt"), None, None, None),
        check_vma=False,
    )
```

profile of v0, /device:TPU:0, one launch (start us, length us, event | category | flops | bytes accessed | tf_op | source)
XLA Modules:
  0.0 75.4 jit_solution(9164925618644152126)
XLA Ops:
  0.0 73.2 %shard_map.37 = bf16[2,2,256,512]{3,2,1,0:T(8,128)(2,1)} custom-call(bf16[2,2,1024,512]{3,2,1,0:T(8,128)(2,1)} %inputs.1, bf16[2,512,1024]{2,1,0:T(8,128)(2,1)} %bitcast.3, bf16[4,2,2,512,256]{4,3,2,1,0:T(8,128)(2,1)} %bitcast.2), custom_call_target="tpu_custom_call" | custom-call | tf_op jit(solution)/shard_map/pallas_call | solution.py:265
  73.2 2.3 %copy.5 = bf16[2,2,256,512]{3,2,1,0:T(8,128)(2,1)} copy(bf16[2,2,256,512]{3,2,1,0:T(8,128)(2,1)} %shard_map.37) | data formatting | bytes 2097152
where the time goes:
time: 75.6 us; the launch traced here: 75.4 us
  Pallas kernels  73.2 us (97%)
  local copies, waits for them, and re-layouts  2.26 us (3%)
    pallas_call x1, Pallas kernels, local(): pl.pallas_call(functools.partial(kernel, (src_bits, tgt_bits, levels, chu...  73.2 us
    unnamed x1, local copies, waits for them, and re-layouts  2.26 us

commit v1 on v0

--- a/solution.py
+++ b/solution.py
@@ -9,6 +9,7 @@
 
 MESH = pl.DeviceIdType.MESH
 LANES = 128
+LAG = 2
 
 
 def product(blocks, vectors):
@@ -30,9 +31,8 @@
     maps,
     blocks,
     coeffs,
+    local_term,
     send1,
-    relay_a,
-    relay_b,
     recv1,
     send2,
     recv2,
@@ -44,10 +44,6 @@
     blocks_sem,
     out_sem,
     s1_sem,
-    ra_sem,
-    rb_sem,
-    fa_sem,
-    fb_sem,
     r1_sem,
     s2_sem,
     r2_sem,
@@ -60,16 +56,14 @@
     hi, lo = 2 ** (src_bits - 1), 2 ** (src_bits - 2)
     far = 2 ** (tgt_bits - 1)
     bit1, bit2, bit3 = src // hi % 2, src // lo % 2, tgt // far % 2
-    flip_lo = src + lo - 2 * lo * bit2
-    flip_both = flip_lo + hi - 2 * hi * bit1
-    near = (flip_lo, tgt)
-    across = (flip_both, tgt)
+    across = (src + hi - 2 * hi * bit1, tgt)
+    near = (src + lo - 2 * lo * bit2, tgt)
     side = (src, tgt + far - 2 * far * bit3)
     is_end = bit1 == bit2
     is_mid = bit1 != bit2
 
     barrier = pltpu.get_barrier_semaphore()
-    for peer in (near, across, side):
+    for peer in (across, near, side):
         pl.semaphore_signal(barrier, inc=1, device_id=peer, device_id_type=MESH)
 
     def load_in(c, n, part):
@@ -108,29 +102,14 @@
             device_id_type=MESH,
         )
 
-    def own_a(u):
-        return remote(send1.at[u], relay_a.at[u], s1_sem.at[u], ra_sem.at[u], near)
-
-    def own_b(u):
-        return remote(send1.at[u], relay_b.at[u], s1_sem.at[u], rb_sem.at[u], across)
-
-    def forward_a(u):
-        return remote(relay_a.at[u], recv1.at[u], fa_sem.at[u], r1_sem.at[u], across)
-
-    def forward_b(u):
-        return remote(relay_b.at[u], recv1.at[u], fb_sem.at[u], r1_sem.at[u], near)
+    def first(u):
+        return remote(send1.at[u], recv1.at[u], s1_sem.at[u], r1_sem.at[u], across)
 
     def second(u):
         return remote(send2.at[u], recv2.at[u], s2_sem.at[u], r2_sem.at[u], near)
 
     def third(u):
         return remote(send3.at[u], recv3.at[u], s3_sem.at[u], r3_sem.at[u], side)
-
-    def forward(u):
-        own_b(u).wait_recv()
-        forward_b(u).start()
-        own_a(u).wait_recv()
-        forward_a(u).start()
 
     def store(u, part):
         return pltpu.make_async_copy(
@@ -164,37 +143,22 @@
                 def _():
                     pl.semaphore_wait(barrier, 3)
 
-            @pl.when(is_end)
-            def _():
-                own_a(u).start()
-
-            @pl.when(is_mid)
-            def _():
-                own_b(u).start()
-
-    def level(v, u, bit, arrived):
-        local_term = product(blocks[v, u % 2, bit], coeffs[u])
-        return (local_term + arrived[u].astype(jnp.float32)).astype(jnp.bfloat16)
-
-    def post1(u):
-        forward_a(u).wait_recv()
-        updated = level(1, u, bit1, recv1)
-        coeffs[u] = updated
+            first(u).start()
+
+    def plus(local_value, arrived):
+        return (local_value + arrived.astype(jnp.float32)).astype(jnp.bfloat16)
+
+    def finish1(u, updated):
         send2[u] = product(blocks[2, u % 2, 1 - bit2], updated).astype(jnp.bfloat16)
         second(u).start()
-
-    def post2(u):
+        return product(blocks[2, u % 2, bit2], updated)
+
+    def finish2(u, local_value):
         second(u).wait_recv()
-        updated = level(2, u, bit2, recv2)
-        coeffs[u] = updated
+        updated = plus(local_value, recv2[u])
         send3[u] = product(blocks[3, u % 2, 1 - bit3], updated).astype(jnp.bfloat16)
         third(u).start()
-
-    def post3(u):
-        third(u).wait_recv()
-        result[u] = level(3, u, bit3, recv3)
-        for part in range(2):
-            store(u, part).start()
+        local_term[u] = product(blocks[3, u % 2, bit3], updated)
 
     for n in range(2):
         load_maps(n).wait()
@@ -203,51 +167,49 @@
     def _(c):
         pre(c)
 
-        @pl.when(jnp.logical_and(is_mid, c > 0))
-        def _():
-            forward(c - 1)
-
     for v in range(2, levels):
         load_blocks(v).wait()
-
-    @pl.when(is_mid)
-    def _():
-        @pl.loop(chunks - 1, units)
-        def _(u):
-            forward(u)
 
     @pl.when(is_end)
     def _():
         @pl.loop(0, units)
         def _(u):
-            post1(u)
-
-    @pl.loop(0, units + 2)
+            local_term[u] = product(blocks[1, u % 2, bit1], coeffs[u])
+
+    @pl.when(is_mid)
+    def _():
+        @pl.loop(0, units)
+        def _(u):
+            local_value = product(blocks[1, u % 2, bit1], coeffs[u])
+            first(u).wait_recv()
+            local_term[u] = finish1(u, plus(local_value, recv1[u]))
+
+    @pl.loop(0, units + LAG)
     def _(u):
+        @pl.when(jnp.logical_and(is_end, u < units))
+        def _():
+            first(u).wait_recv()
+            finish2(u, finish1(u, plus(local_term[u], recv1[u])))
+
         @pl.when(jnp.logical_and(is_mid, u < units))
         def _():
-            post1(u)
-
-        @pl.when(jnp.logical_and(u >= 1, u < units + 1))
-        def _():
-            post2(u - 1)
-
-        @pl.when(u >= 2)
-        def _():
-            post3(u - 2)
+            finish2(u, local_term[u])
+
+        @pl.when(u >= LAG)
+        def _():
+            w = u - LAG
+            third(w).wait_recv()
+            result[w] = plus(local_term[w], recv3[w])
+            for part in range(2):
+                store(w, part).start()
 
     @pl.loop(0, units)
     def _(u):
-        own_a(u).wait_send()
+        first(u).wait_send()
         second(u).wait_send()
         third(u).wait_send()
         for part in range(2):
             store(u, part).wait()
-
-        @pl.when(is_mid)
-        def _():
-            forward_a(u).wait_send()
-            forward_b(u).wait_send()
 
 
 def local(inputs, leaf_maps, transfer_blocks):
@@ -271,15 +233,17 @@
             pltpu.VMEM((chunks, nodes, depth, 2 * LANES), jnp.bfloat16),
             pltpu.VMEM(maps.shape, jnp.bfloat16),
             pltpu.VMEM(blocks.shape, jnp.bfloat16),
+            unit,
+            pltpu.VMEM((units, rank, 2 * LANES), jnp.float32),
         ]
-        + [unit] * 10
+        + [unit] * 7
         + [
             dma((chunks, nodes, 2)),
             dma((nodes,)),
             dma((levels,)),
             dma((units, 2)),
         ]
-        + [dma((units,))] * 10,
+        + [dma((units,))] * 6,
         compiler_params=pltpu.CompilerParams(
             collective_id=0, has_side_effects=True, vmem_limit_bytes=60 * 2**20
         ),

time: 75.6 us -> 73.1 us (0.967)
  the two profiles are of different devices: /device:TPU:0 before, /device:TPU:16 now
where the time goes in v1:
time: 73.1 us; the launch traced here: 72.9 us
  Pallas kernels  70.7 us (97%)
  local copies, waits for them, and re-layouts  2.26 us (3%)
    pallas_call x1, Pallas kernels, local(): pl.pallas_call(functools.partial(kernel, (src_bits, tgt_bits, levels, chu...  70.7 us
    unnamed x1, local copies, waits for them, and re-layouts  2.26 us

profile of v1, /device:TPU:16, one launch (start us, length us, event | category | flops | bytes accessed | tf_op | source)
XLA Modules:
  0.0 72.9 jit_solution(4341740870745655828)
XLA Ops:
  0.0 70.7 %shard_map.37 = bf16[2,2,256,512]{3,2,1,0:T(8,128)(2,1)} custom-call(bf16[2,2,1024,512]{3,2,1,0:T(8,128)(2,1)} %inputs.1, bf16[2,512,1024]{2,1,0:T(8,128)(2,1)} %bitcast.3, bf16[4,2,2,512,256]{4,3,2,1,0:T(8,128)(2,1)} %bitcast.2), custom_call_target="tpu_custom_call" | custom-call | tf_op jit(solution)/shard_map/pallas_call | solution.py:227
  70.7 2.3 %copy.5 = bf16[2,2,256,512]{3,2,1,0:T(8,128)(2,1)} copy(bf16[2,2,256,512]{3,2,1,0:T(8,128)(2,1)} %shard_map.37) | data formatting | bytes 2097152

commit v2 on v1

v2 whole, which is shorter than its diff:
```python
import functools

import jax
import jax.numpy as jnp
from jax import lax
from jax.experimental import pallas as pl
from jax.experimental.pallas import tpu as pltpu
from jax.sharding import PartitionSpec as P

MESH = pl.DeviceIdType.MESH
LANES = 128
HALF = LANES // 2
AHEAD = 4
LIMIT = 60
LEAD = 4
LAG2 = 3
LAG3 = 2


def low_lanes(shape):
    return lax.broadcasted_iota(jnp.int32, shape, 1) < HALF


def times_i(slot):
    turned = pltpu.roll(slot, HALF, 1)
    return jnp.where(low_lanes(slot.shape), -turned, turned)


def stacked(slot):
    rounded = slot.astype(jnp.bfloat16)
    return jnp.concatenate([rounded, times_i(slot).astype(jnp.bfloat16)], axis=0)


def dot(left, right):
    return jnp.dot(left, right, preferred_element_type=jnp.float32)


def kernel(
    sizes,
    inputs,
    leaf_maps,
    transfer,
    out,
    x_in,
    maps,
    blocks,
    vectors,
    coeffs,
    local_term,
    send1,
    recv1,
    send2,
    recv2,
    send3,
    recv3,
    in_sem,
    maps_sem,
    blocks_sem,
    s1_sem,
    r1_sem,
    s2_sem,
    r2_sem,
    s3_sem,
    r3_sem,
):
    src_bits, tgt_bits, levels, chunks = sizes
    items = 4 * chunks
    rank = maps.shape[1] // 2
    src, tgt = lax.axis_index("src"), lax.axis_index("tgt")
    hi, lo = 2 ** (src_bits - 1), 2 ** (src_bits - 2)
    far = 2 ** (tgt_bits - 1)
    bit1, bit2, bit3 = src // hi % 2, src // lo % 2, tgt // far % 2
    across = (src + hi - 2 * hi * bit1, tgt)
    near = (src + lo - 2 * lo * bit2, tgt)
    side = (src, tgt + far - 2 * far * bit3)
    is_end = bit1 == bit2
    is_mid = bit1 != bit2

    barrier = pltpu.get_barrier_semaphore()
    for peer in (across, near, side):
        pl.semaphore_signal(barrier, inc=1, device_id=peer, device_id_type=MESH)

    def load_in(c, n, part):
        return pltpu.make_async_copy(
            inputs.at[n, part, :, pl.ds(pl.multiple_of(c * LANES, LANES), LANES)],
            x_in.at[c, n, :, pl.ds(part * LANES, LANES)],
            in_sem.at[c, n, part],
        )

    def load_maps(n):
        return pltpu.make_async_copy(leaf_maps.at[n], maps.at[n], maps_sem.at[n])

    def load_blocks(v, k, part):
        return pltpu.make_async_copy(
            transfer.at[v, :, k, part],
            blocks.at[v, :, k, :, pl.ds(part * rank, rank)],
            blocks_sem.at[v, k, part],
        )

    def start_in(c):
        for n in range(2):
            for part in range(2):
                load_in(c, n, part).start()

    def start_blocks(v, k):
        for part in range(2):
            load_blocks(v, k, part).start()

    def wait_blocks(v, k):
        for part in range(2):
            load_blocks(v, k, part).wait()

    for n in range(2):
        load_maps(n).start()
        for part in range(2):
            load_in(0, n, part).start()
    for k in range(2):
        start_blocks(0, k)
    start_blocks(1, 1 - bit1)

    def remote(source, target, send_sem, recv_sem, peer):
        return pltpu.make_async_remote_copy(
            src_ref=source,
            dst_ref=target,
            send_sem=send_sem,
            recv_sem=recv_sem,
            device_id=peer,
            device_id_type=MESH,
        )

    def first(i):
        return remote(send1.at[i], recv1.at[i], s1_sem.at[i], r1_sem.at[i], across)

    def second(i):
        return remote(send2.at[i], recv2.at[i], s2_sem.at[i], r2_sem.at[i], near)

    def third(i):
        return remote(send3.at[i], recv3.at[i], s3_sem.at[i], r3_sem.at[i], side)

    def leaf(c, n):
        both = dot(maps[n], x_in[c, n])
        real_part = both[:rank, :LANES] - both[rank:, LANES:]
        imag_part = both[:rank, LANES:] + both[rank:, :LANES]
        low = low_lanes(real_part.shape)
        slots = (
            jnp.where(low, real_part, pltpu.roll(imag_part, HALF, 1)),
            jnp.where(low, pltpu.roll(real_part, HALF, 1), imag_part),
        )
        return jnp.concatenate([stacked(slot) for slot in slots], axis=1)

    def leaves(c):
        for n in range(2):

            @pl.when(c == 0)
            def _():
                load_maps(n).wait()

            for part in range(2):
                load_in(c, n, part).wait()

            @pl.when(c == 0)
            def _():
                start_in(n + 1)

            vectors[n] = leaf(c, n)

    def spread(c):
        @pl.when(c == 0)
        def _():
            for k in range(2):
                wait_blocks(0, k)
            start_blocks(1, bit1)
            for v in range(2, levels):
                for k in range(2):
                    start_blocks(v, k)
            for w in range(3, chunks):
                start_in(w)
            wait_blocks(1, 1 - bit1)

        for n in range(2):
            updated = dot(blocks[0, n, n], vectors[n]) + dot(
                blocks[0, 1 - n, n], vectors[1 - n]
            )
            slots = [
                stacked(updated[:, h * LANES : (h + 1) * LANES]) for h in range(2)
            ]
            sent = dot(
                blocks[1, n, 1 - bit1], jnp.concatenate(slots, axis=1)
            ).astype(jnp.bfloat16)
            for h in range(2):
                i = 4 * c + 2 * n + h
                coeffs[i] = slots[h]
                send1[i] = sent[:, h * LANES : (h + 1) * LANES]
            for h in range(2):
                i = 4 * c + 2 * n + h

                @pl.when(jnp.logical_or(is_mid, i < AHEAD))
                def _():
                    first(i).start()

    def one(i):
        n = i // 2 % 2
        own = dot(blocks[1, n, bit1], coeffs[i])
        first(i).wait_recv()
        slot = stacked(own + recv1[i].astype(jnp.float32))
        send2[i] = dot(blocks[2, n, 1 - bit2], slot).astype(jnp.bfloat16)
        second(i).start()

        local_term[i] = dot(blocks[2, n, bit2], slot)

    def two(i):
        n = i // 2 % 2
        second(i).wait_recv()
        slot = stacked(local_term[i] + recv2[i].astype(jnp.float32))
        send3[i] = dot(blocks[3, n, 1 - bit3], slot).astype(jnp.bfloat16)
        third(i).start()
        local_term[i] = dot(blocks[3, n, bit3], slot)

    def three(j):
        slots = []
        for h in range(2):
            i = 2 * j + h
            third(i).wait_recv()
            slots.append(local_term[i] + recv3[i].astype(jnp.float32))
        low = low_lanes(slots[0].shape)
        real_part = jnp.where(low, slots[0], pltpu.roll(slots[1], HALF, 1))
        imag_part = jnp.where(low, pltpu.roll(slots[0], HALF, 1), slots[1])
        columns = pl.ds(pl.multiple_of(j // 2 * LANES, LANES), LANES)
        out[j % 2, 0, :, columns] = real_part.astype(jnp.bfloat16)
        out[j % 2, 1, :, columns] = imag_part.astype(jnp.bfloat16)

    pl.semaphore_wait(barrier, 3)

    @pl.loop(0, items + LEAD + LAG2 + LAG3)
    def _(t):
        i = t - LEAD

        @pl.when(jnp.logical_and(i >= 0, i < items))
        def _():
            one(i)

        @pl.when(jnp.logical_and(t % 2 == 0, t < 2 * chunks))
        def _():
            leaves(t // 2)

        @pl.when(jnp.logical_and(t % 2 == 1, t < 2 * chunks))
        def _():
            spread(t // 2)

        ahead = i + AHEAD

        @pl.when(jnp.logical_and(is_end, jnp.logical_and(i >= 0, ahead < items)))
        def _():
            first(ahead).start()

        @pl.when(t == 1)
        def _():
            wait_blocks(1, bit1)
            for v in range(2, levels):
                for k in range(2):
                    wait_blocks(v, k)

        @pl.when(jnp.logical_and(i >= LAG2, i < items + LAG2))
        def _():
            two(i - LAG2)

        done = i - LAG2 - LAG3

        @pl.when(jnp.logical_and(done >= 0, done % 2 == 1))
        def _():
            three(done // 2)

    @pl.loop(0, items)
    def _(i):
        first(i).wait_send()
        second(i).wait_send()
        third(i).wait_send()


def local(inputs, leaf_maps, transfer_blocks):
    nodes, _, depth, columns = inputs.shape
    rank = leaf_maps.shape[2]
    levels = transfer_blocks.shape[0]
    chunks = columns // LANES
    items = 2 * nodes * chunks
    src_bits = lax.axis_size("src").bit_length() - 1
    tgt_bits = lax.axis_size("tgt").bit_length() - 1
    maps = leaf_maps.reshape(nodes, 2 * rank, depth)
    slots = pltpu.VMEM((items, rank, LANES), jnp.bfloat16)
    dma = pltpu.SemaphoreType.DMA
    return pl.pallas_call(
        functools.partial(kernel, (src_bits, tgt_bits, levels, chunks)),
        out_shape=pltpu.VMEM((nodes, 2, rank, columns), jnp.bfloat16),
        in_specs=[pl.BlockSpec(memory_space=pl.ANY)] * 3,
        out_specs=pl.BlockSpec(memory_space=pltpu.VMEM),
        scratch_shapes=[
            pltpu.VMEM((chunks, nodes, depth, 2 * LANES), jnp.bfloat16),
            pltpu.VMEM(maps.shape, jnp.bfloat16),
            pltpu.VMEM((levels, nodes, 2, rank, 2 * rank), jnp.bfloat16),
            pltpu.VMEM((nodes, 2 * rank, 2 * LANES), jnp.bfloat16),
            pltpu.VMEM((items, 2 * rank, LANES), jnp.bfloat16),
            pltpu.VMEM((items, rank, LANES), jnp.float32),
        ]
        + [slots] * 6
        + [
            dma((chunks, nodes, 2)),
            dma((nodes,)),
            dma((levels, 2, 2)),
        ]
        + [dma((items,))] * 6,
        compiler_params=pltpu.CompilerParams(
            collective_id=0, has_side_effects=True, vmem_limit_bytes=LIMIT * 2**20
        ),
    )(inputs, maps, transfer_blocks)


def solution(mesh):
    placed = (
        P(("src", "tgt"), None, None, None),
        P(("src", "tgt"), None, None, None),
        P(None, ("src", "tgt"), None, None, None, None),
    )
    return jax.shard_map(
        local,
        mesh=mesh,
        in_specs=placed,
        out_specs=P(("src", "tgt"), None, None, None),
        check_vma=False,
    )
```

time: 73.1 us -> 64.5 us (0.88)
  the two profiles are of different devices: /device:TPU:16 before, /device:TPU:0 now
where the time goes in v2:
time: 64.5 us; the launch traced here: 64.4 us
  Pallas kernels  63.4 us (98%)
  local copies, waits for them, and re-layouts  0.97 us (2%)
    pallas_call x1, Pallas kernels, local(): pl.pallas_call(functools.partial(kernel, (src_bits, tgt_bits, levels, chu...  63.4 us

profile of v2, /device:TPU:0, one launch (start us, length us, event | category | flops | bytes accessed | tf_op | source)
XLA Modules:
  0.0 64.4 jit_solution(4251729981544656705)
XLA Ops:
  0.0 63.4 %shard_map.37 = bf16[2,2,256,512]{3,2,1,0:T(8,128)(2,1)S(1)} custom-call(bf16[2,2,1024,512]{3,2,1,0:T(8,128)(2,1)} %inputs.1, bf16[2,512,1024]{2,1,0:T(8,128)(2,1)} %bitcast.1, bf16[4,2,2,2,256,256]{5,4,3,2,1,0:T(8,128)(2,1)} %transfer.1), custom_call_target="tpu_custom_call" | custom-call | tf_op jit(solution)/shard_map/pallas_call | solution.py:291
  63.4 1.0 %copy.5 = bf16[2,2,256,512]{3,2,1,0:T(8,128)(2,1)} copy(bf16[2,2,256,512]{3,2,1,0:T(8,128)(2,1)S(1)} %shard_map.37) | data formatting | bytes 2097152

commit v3 on v2

--- a/solution.py
+++ b/solution.py
@@ -43,9 +43,9 @@
     out,
     x_in,
     maps,
+    mix,
     blocks,
     vectors,
-    coeffs,
     local_term,
     send1,
     recv1,
@@ -55,6 +55,7 @@
     recv3,
     in_sem,
     maps_sem,
+    mix_sem,
     blocks_sem,
     s1_sem,
     r1_sem,
@@ -90,9 +91,17 @@
     def load_maps(n):
         return pltpu.make_async_copy(leaf_maps.at[n], maps.at[n], maps_sem.at[n])
 
+    def load_mix(m, part):
+        return pltpu.make_async_copy(
+            transfer.at[0, m, :, part],
+            mix.at[:, :, pl.ds((2 * m + part) * rank, rank)],
+            mix_sem.at[m, part],
+        )
+
     def load_blocks(v, k, part):
+        bit = (bit1, bit2, bit3)[v]
         return pltpu.make_async_copy(
-            transfer.at[v, :, k, part],
+            transfer.at[v + 1, :, bit if k else 1 - bit, part],
             blocks.at[v, :, k, :, pl.ds(part * rank, rank)],
             blocks_sem.at[v, k, part],
         )
@@ -114,9 +123,11 @@
         load_maps(n).start()
         for part in range(2):
             load_in(0, n, part).start()
+    for m in range(2):
+        for part in range(2):
+            load_mix(m, part).start()
     for k in range(2):
         start_blocks(0, k)
-    start_blocks(1, 1 - bit1)
 
     def remote(source, target, send_sem, recv_sem, peer):
         return pltpu.make_async_remote_copy(
@@ -142,11 +153,23 @@
         real_part = both[:rank, :LANES] - both[rank:, LANES:]
         imag_part = both[:rank, LANES:] + both[rank:, :LANES]
         low = low_lanes(real_part.shape)
+        real_turned = pltpu.roll(real_part, HALF, 1)
+        imag_turned = pltpu.roll(imag_part, HALF, 1)
         slots = (
-            jnp.where(low, real_part, pltpu.roll(imag_part, HALF, 1)),
-            jnp.where(low, pltpu.roll(real_part, HALF, 1), imag_part),
-        )
-        return jnp.concatenate([stacked(slot) for slot in slots], axis=1)
+            jnp.where(low, real_part, imag_turned),
+            jnp.where(low, real_turned, imag_part),
+        )
+        turned = (
+            jnp.where(low, -imag_part, real_turned),
+            jnp.where(low, -imag_turned, real_part),
+        )
+        return jnp.concatenate(
+            [
+                jnp.concatenate([part.astype(jnp.bfloat16) for part in both], axis=1)
+                for both in (slots, turned)
+            ],
+            axis=0,
+        )
 
     def leaves(c):
         for n in range(2):
@@ -162,59 +185,61 @@
             def _():
                 start_in(n + 1)
 
-            vectors[n] = leaf(c, n)
+            vectors[pl.ds(2 * rank * n, 2 * rank)] = leaf(c, n)
 
     def spread(c):
         @pl.when(c == 0)
         def _():
-            for k in range(2):
-                wait_blocks(0, k)
-            start_blocks(1, bit1)
-            for v in range(2, levels):
+            for m in range(2):
+                for part in range(2):
+                    load_mix(m, part).wait()
+            for v in range(1, levels - 1):
                 for k in range(2):
                     start_blocks(v, k)
             for w in range(3, chunks):
                 start_in(w)
-            wait_blocks(1, 1 - bit1)
+            wait_blocks(0, 0)
 
         for n in range(2):
-            updated = dot(blocks[0, n, n], vectors[n]) + dot(
-                blocks[0, 1 - n, n], vectors[1 - n]
+            updated = dot(mix[n], vectors[...])
+            slots = jnp.concatenate(
+                [stacked(updated[:, h * LANES : (h + 1) * LANES]) for h in range(2)],
+                axis=1,
             )
-            slots = [
-                stacked(updated[:, h * LANES : (h + 1) * LANES]) for h in range(2)
-            ]
-            sent = dot(
-                blocks[1, n, 1 - bit1], jnp.concatenate(slots, axis=1)
-            ).astype(jnp.bfloat16)
+            sent = dot(blocks[0, n, 0], slots).astype(jnp.bfloat16)
             for h in range(2):
                 i = 4 * c + 2 * n + h
-                coeffs[i] = slots[h]
                 send1[i] = sent[:, h * LANES : (h + 1) * LANES]
-            for h in range(2):
-                i = 4 * c + 2 * n + h
 
                 @pl.when(jnp.logical_or(is_mid, i < AHEAD))
                 def _():
                     first(i).start()
 
+            if n == 0:
+
+                @pl.when(c == 0)
+                def _():
+                    wait_blocks(0, 1)
+
+            own = dot(blocks[0, n, 1], slots)
+            for h in range(2):
+                local_term[4 * c + 2 * n + h] = own[:, h * LANES : (h + 1) * LANES]
+
     def one(i):
         n = i // 2 % 2
-        own = dot(blocks[1, n, bit1], coeffs[i])
         first(i).wait_recv()
-        slot = stacked(own + recv1[i].astype(jnp.float32))
-        send2[i] = dot(blocks[2, n, 1 - bit2], slot).astype(jnp.bfloat16)
+        slot = stacked(local_term[i] + recv1[i].astype(jnp.float32))
+        send2[i] = dot(blocks[1, n, 0], slot).astype(jnp.bfloat16)
         second(i).start()
-
-        local_term[i] = dot(blocks[2, n, bit2], slot)
+        local_term[i] = dot(blocks[1, n, 1], slot)
 
     def two(i):
         n = i // 2 % 2
         second(i).wait_recv()
         slot = stacked(local_term[i] + recv2[i].astype(jnp.float32))
-        send3[i] = dot(blocks[3, n, 1 - bit3], slot).astype(jnp.bfloat16)
+        send3[i] = dot(blocks[2, n, 0], slot).astype(jnp.bfloat16)
         third(i).start()
-        local_term[i] = dot(blocks[3, n, bit3], slot)
+        local_term[i] = dot(blocks[2, n, 1], slot)
 
     def three(j):
         slots = []
@@ -255,8 +280,7 @@
 
         @pl.when(t == 1)
         def _():
-            wait_blocks(1, bit1)
-            for v in range(2, levels):
+            for v in range(1, levels - 1):
                 for k in range(2):
                     wait_blocks(v, k)
 
@@ -296,16 +320,17 @@
         scratch_shapes=[
             pltpu.VMEM((chunks, nodes, depth, 2 * LANES), jnp.bfloat16),
             pltpu.VMEM(maps.shape, jnp.bfloat16),
-            pltpu.VMEM((levels, nodes, 2, rank, 2 * rank), jnp.bfloat16),
-            pltpu.VMEM((nodes, 2 * rank, 2 * LANES), jnp.bfloat16),
-            pltpu.VMEM((items, 2 * rank, LANES), jnp.bfloat16),
+            pltpu.VMEM((nodes, rank, 2 * nodes * rank), jnp.bfloat16),
+            pltpu.VMEM((levels - 1, nodes, 2, rank, 2 * rank), jnp.bfloat16),
+            pltpu.VMEM((2 * nodes * rank, 2 * LANES), jnp.bfloat16),
             pltpu.VMEM((items, rank, LANES), jnp.float32),
         ]
         + [slots] * 6
         + [
             dma((chunks, nodes, 2)),
             dma((nodes,)),
-            dma((levels, 2, 2)),
+            dma((nodes, 2)),
+            dma((levels - 1, 2, 2)),
         ]
         + [dma((items,))] * 6,
         compiler_params=pltpu.CompilerParams(

time: 64.5 us -> 64.3 us (level)
  no operation moved by 1% of the time
where the time goes in v3:
time: 64.3 us; the launch traced here: 64.1 us
  Pallas kernels  63.2 us (98%)
  local copies, waits for them, and re-layouts  0.97 us (2%)
    pallas_call x1, Pallas kernels, local(): pl.pallas_call(functools.partial(kernel, (src_bits, tgt_bits, levels, chu...  63.2 us

profile of v3, /device:TPU:0, one launch (start us, length us, event | category | flops | bytes accessed | tf_op | source)
XLA Modules:
  0.0 64.1 jit_solution(4677123818006829534)
XLA Ops:
  0.0 63.2 %shard_map.37 = bf16[2,2,256,512]{3,2,1,0:T(8,128)(2,1)S(1)} custom-call(bf16[2,2,1024,512]{3,2,1,0:T(8,128)(2,1)} %inputs.1, bf16[2,512,1024]{2,1,0:T(8,128)(2,1)} %bitcast.1, bf16[4,2,2,2,256,256]{5,4,3,2,1,0:T(8,128)(2,1)} %transfer.1), custom_call_target="tpu_custom_call" | custom-call | tf_op jit(solution)/shard_map/pallas_call | solution.py:315
  63.2 1.0 %copy.5 = bf16[2,2,256,512]{3,2,1,0:T(8,128)(2,1)} copy(bf16[2,2,256,512]{3,2,1,0:T(8,128)(2,1)S(1)} %shard_map.37) | data formatting | bytes 2097152

commit v4 on v3

--- a/solution.py
+++ b/solution.py
@@ -12,7 +12,7 @@
 HALF = LANES // 2
 AHEAD = 4
 LIMIT = 60
-LEAD = 4
+LEAD = 3
 LAG2 = 3
 LAG3 = 2
 
@@ -120,9 +120,9 @@
             load_blocks(v, k, part).wait()
 
     for n in range(2):
-        load_maps(n).start()
         for part in range(2):
             load_in(0, n, part).start()
+        load_maps(n).start()
     for m in range(2):
         for part in range(2):
             load_mix(m, part).start()

time: 64.3 us -> 64 us (level)
  no operation moved by 1% of the time
where the time goes in v4:
time: 64 us; the launch traced here: 63.9 us
  Pallas kernels  62.9 us (98%)
  local copies, waits for them, and re-layouts  0.97 us (2%)
    pallas_call x1, Pallas kernels, local(): pl.pallas_call(functools.partial(kernel, (src_bits, tgt_bits, levels, chu...  62.9 us

profile of v4, /device:TPU:0, one launch (start us, length us, event | category | flops | bytes accessed | tf_op | source)
XLA Modules:
  0.0 63.9 jit_solution(3866739764505427394)
XLA Ops:
  0.0 62.9 %shard_map.37 = bf16[2,2,256,512]{3,2,1,0:T(8,128)(2,1)S(1)} custom-call(bf16[2,2,1024,512]{3,2,1,0:T(8,128)(2,1)} %inputs.1, bf16[2,512,1024]{2,1,0:T(8,128)(2,1)} %bitcast.1, bf16[4,2,2,2,256,256]{5,4,3,2,1,0:T(8,128)(2,1)} %transfer.1), custom_call_target="tpu_custom_call" | custom-call | tf_op jit(solution)/shard_map/pallas_call | solution.py:315
  62.9 1.0 %copy.5 = bf16[2,2,256,512]{3,2,1,0:T(8,128)(2,1)} copy(bf16[2,2,256,512]{3,2,1,0:T(8,128)(2,1)S(1)} %shard_map.37) | data formatting | bytes 2097152
